TPU v7x, 32 devices: a whole 2x2x4 slice. The times are simulated.
32 devices in a mesh: ctx: 4 (over y, x), wsh: 8 (over z, core).
Axes of the slice: x: 2, y: 2, z: 4, core: 2. Of those that a mesh axis runs over, the one named last changes fastest.
Arguments:
- tokens: bfloat16 [8, 2048, 768], P('wsh', 'ctx'), may hold values from -6 to 6
- cluster_order: int32 [8, 2048], P('wsh', 'ctx'), may hold values from 0 to 2047, as said below
- qkv_weight: bfloat16 [768, 2304], P('wsh'), may hold values from -0.21875 to 0.21875
- query_bias: bfloat16 [768], P('wsh'), may hold values from -3 to 3
- value_bias: bfloat16 [768], P('wsh'), may hold values from -1.25 to 1.25
- out_weight: bfloat16 [768, 768], P('wsh'), may hold values from -1.25 to 1.25
- out_bias: bfloat16 [768], P('wsh'), may hold values from -1.75 to 1.75
- first_gain: bfloat16 [768], P('wsh'), may hold values from 0.25 to 1.75
- first_shift: bfloat16 [768], P('wsh'), may hold values from -1.75 to 1.75
- up_weight: bfloat16 [768, 3072], P('wsh'), may hold values from -0.21875 to 0.21875
- up_bias: bfloat16 [3072], P('wsh'), may hold values from -3 to 3
- down_weight: bfloat16 [3072, 768], P('wsh'), may hold values from -0.109375 to 0.109375
- down_bias: bfloat16 [768], P('wsh'), may hold values from -1.75 to 1.75
- second_gain: bfloat16 [768], P('wsh'), may hold values from 0.25 to 1.75
- second_shift: bfloat16 [768], P('wsh'), may hold values from -1.75 to 1.75
- cotangent: bfloat16 [8, 2048, 768], P('wsh', 'ctx'), may hold values from -6 to 6
Outputs:
- layer_out: bfloat16 [8, 2048, 768], P('wsh', 'ctx')
- grad_tokens: float32 [8, 2048, 768], P('wsh', 'ctx')
- grad_qkv_weight: float32 [768, 2304], P('wsh')
- grad_query_bias: float32 [768], P('wsh')
- grad_value_bias: float32 [768], P('wsh')
- grad_out_weight: float32 [768, 768], P('wsh')
- grad_out_bias: float32 [768], P('wsh')
- grad_first_gain: float32 [768], P('wsh')
- grad_first_shift: float32 [768], P('wsh')
- grad_up_weight: float32 [768, 3072], P('wsh')
- grad_up_bias: float32 [3072], P('wsh')
- grad_down_weight: float32 [3072, 768], P('wsh')
- grad_down_bias: float32 [768], P('wsh')
- grad_second_gain: float32 [768], P('wsh')
- grad_second_shift: float32 [768], P('wsh')
Inputs may be any that keep to these rules, and one draw needn't show every extreme that they name: `cluster_order`: each stream's row is a permutation of its positions. The stream is cut into four documents, each a multiple of 128 tokens long, the longest exactly 1024; the permutation maps every document's positions onto themselves, so each cluster lies within one document.
All inputs are finite; a program needn't handle non-finite values.
Results may differ from a plain program's by a relative error of at most 0.02.
Values may be sent and summed in bfloat16 or wider, within the bound.
A program may use at most 128 MiB of HBM per device.

v0:
```python
import jax
import jax.numpy as jnp
from jax import lax
from jax.sharding import PartitionSpec as P

HEAD_DIM = 64
CLUSTER = 128
epsilon = 1e-05


def inner(left, right):
    return lax.dot_general(
        left, right, (((0,), (0,)), ((), ())), preferred_element_type=jnp.float32
    )


def times_transposed(left, right):
    return lax.dot_general(
        left, right, (((1,), (1,)), ((), ())), preferred_element_type=jnp.float32
    )


def normalize(values):
    centre = values - jnp.mean(values, axis=1, keepdims=True)
    factor = lax.rsqrt(jnp.mean(centre * centre, axis=1, keepdims=True) + epsilon)
    return (centre * factor, factor)


def norm_back(grad_out, normed, factor, gain):
    grad_normed = grad_out * gain
    return factor * (
        grad_normed
        - jnp.mean(grad_normed, axis=1, keepdims=True)
        - normed * jnp.mean(grad_normed * normed, axis=1, keepdims=True)
    )


def on_device(
    tokens,
    cluster_order,
    qkv_weight,
    query_bias,
    value_bias,
    out_weight,
    out_bias,
    first_gain,
    first_shift,
    up_weight,
    up_bias,
    down_weight,
    down_bias,
    second_gain,
    second_shift,
    cotangent,
):
    order = cluster_order[0]
    rows = tokens.shape[1]
    width = tokens.shape[2]
    heads = width // HEAD_DIM
    blocks = rows // CLUSTER
    group_rows = rows * lax.axis_size("ctx")
    first_row = lax.axis_index("ctx") * rows
    factor_qk = HEAD_DIM ** (-0.5)
    small = [
        query_bias,
        value_bias,
        out_bias,
        first_gain,
        first_shift,
        down_bias,
        second_gain,
        second_shift,
        up_bias,
    ]
    sizes = [v.shape[0] for v in small]
    packed = lax.all_gather(jnp.concatenate(small), "wsh", axis=0, tiled=False)
    spots = [sum(sizes[:i]) for i in range(len(sizes))]
    qbias, vbias, obias, gain_one, shift_one, dbias, gain_two, shift_two, ubias = [
        packed[:, s : s + n].reshape(-1).astype(jnp.float32) for s, n in zip(spots, sizes)
    ]
    whole_order = lax.all_gather(order, "ctx", axis=0, tiled=True)
    both = lax.all_gather(
        jnp.concatenate([tokens[0], cotangent[0]], axis=1), "ctx", axis=0, tiled=True
    )
    whole_qkv = lax.all_gather(qkv_weight, "wsh", axis=0, tiled=True)
    whole_out = lax.all_gather(out_weight, "wsh", axis=0, tiled=True)
    whole_up = lax.all_gather(up_weight, "wsh", axis=0, tiled=True)
    whole_down = lax.all_gather(down_weight, "wsh", axis=0, tiled=True)
    take = (order[:, None] == jnp.arange(group_rows, dtype=jnp.int32)[None, :]).astype(jnp.bfloat16)
    home = (
        (first_row + jnp.arange(rows, dtype=jnp.int32))[:, None] == whole_order[None, :]
    ).astype(jnp.bfloat16)
    mine = jnp.dot(take, both, preferred_element_type=jnp.float32)
    inputs = mine[:, :width].astype(jnp.bfloat16)
    grad_top = mine[:, width:]
    qkv_shift = jnp.concatenate([qbias, jnp.zeros((width,), jnp.float32), vbias])
    own_qkv = (jnp.dot(inputs, whole_qkv, preferred_element_type=jnp.float32) + qkv_shift).astype(
        jnp.bfloat16
    )
    query = own_qkv[:, :width].reshape(blocks, CLUSTER, heads, HEAD_DIM)
    keyed = own_qkv[:, width : 2 * width].reshape(blocks, CLUSTER, heads, HEAD_DIM)
    valued = own_qkv[:, 2 * width :].reshape(blocks, CLUSTER, heads, HEAD_DIM)
    places = order.reshape(blocks, CLUSTER)
    visible = (places[:, None, :] <= places[:, :, None])[:, None, :, :]
    scores = (
        jnp.einsum("cihd,cjhd->chij", query, keyed, preferred_element_type=jnp.float32) * factor_qk
    )
    masked = jnp.where(visible, scores, -1e30)
    row_max = jnp.max(masked, axis=3, keepdims=True)
    expd = jnp.where(visible, jnp.exp(masked - row_max), 0.0)
    total = jnp.sum(expd, axis=3, keepdims=True)
    probs_full = expd / total
    probs = probs_full.astype(jnp.bfloat16)
    context = (
        jnp.einsum("chij,cjhd->cihd", probs, valued, preferred_element_type=jnp.float32)
        .astype(jnp.bfloat16)
        .reshape(rows, width)
    )
    attended = (
        (jnp.dot(context, whole_out, preferred_element_type=jnp.float32) + obias)
        .astype(jnp.bfloat16)
        .astype(jnp.float32)
    )
    resid = inputs.astype(jnp.float32) + attended
    first_norm, first_factor = normalize(resid)
    first_out = first_norm * gain_one + shift_one
    first_low = first_out.astype(jnp.bfloat16)
    pre_act = jnp.dot(first_low, whole_up, preferred_element_type=jnp.float32) + ubias
    half = 0.5 * (1.0 + lax.erf(pre_act * 0.7071067811865476))
    hidden = (pre_act * half).astype(jnp.bfloat16)
    slope = half + pre_act * jnp.exp(-0.5 * pre_act * pre_act) * 0.3989422804014327
    second_in = first_out + jnp.dot(hidden, whole_down, preferred_element_type=jnp.float32) + dbias
    second_norm, second_factor = normalize(second_in)
    layer_out = (second_norm * gain_two + shift_two).astype(jnp.bfloat16)
    group_out = lax.all_gather(layer_out, "ctx", axis=0, tiled=True)
    out_home = jnp.dot(home, group_out, preferred_element_type=jnp.float32).astype(jnp.bfloat16)
    grad_gain_two = jnp.sum(grad_top * second_norm, axis=0)
    grad_shift_two = jnp.sum(grad_top, axis=0)
    grad_second = norm_back(grad_top, second_norm, second_factor, gain_two)
    grad_branch2 = grad_second.astype(jnp.bfloat16)
    grad_down_w = inner(hidden, grad_branch2).astype(jnp.bfloat16)
    grad_down_b = jnp.sum(grad_branch2.astype(jnp.float32), axis=0)
    grad_hidden = times_transposed(grad_branch2, whole_down)
    grad_pre = (grad_hidden * slope).astype(jnp.bfloat16)
    grad_up_w = inner(first_low, grad_pre).astype(jnp.bfloat16)
    grad_up_b = jnp.sum(grad_pre.astype(jnp.float32), axis=0)
    grad_first = grad_second + times_transposed(grad_pre, whole_up)
    grad_gain_one = jnp.sum(grad_first * first_norm, axis=0)
    grad_shift_one = jnp.sum(grad_first, axis=0)
    grad_resid = norm_back(grad_first, first_norm, first_factor, gain_one)
    grad_attended = grad_resid.astype(jnp.bfloat16)
    grad_out_b = jnp.sum(grad_attended.astype(jnp.float32), axis=0)
    grad_out_w = inner(context, grad_attended).astype(jnp.bfloat16)
    grad_context = (
        times_transposed(grad_attended, whole_out)
        .astype(jnp.bfloat16)
        .reshape(blocks, CLUSTER, heads, HEAD_DIM)
    )
    grad_probs = jnp.einsum(
        "cihd,cjhd->chij", grad_context, valued, preferred_element_type=jnp.float32
    )
    grad_valued = jnp.einsum(
        "chij,cihd->cjhd", probs, grad_context, preferred_element_type=jnp.float32
    ).astype(jnp.bfloat16)
    inner_sum = jnp.sum(probs_full * grad_probs, axis=3, keepdims=True)
    grad_scores = (probs_full * (grad_probs - inner_sum)).astype(jnp.bfloat16)
    grad_query = (
        jnp.einsum("chij,cjhd->cihd", grad_scores, keyed, preferred_element_type=jnp.float32)
        * factor_qk
    ).astype(jnp.bfloat16)
    grad_keyed = (
        jnp.einsum("chij,cihd->cjhd", grad_scores, query, preferred_element_type=jnp.float32)
        * factor_qk
    ).astype(jnp.bfloat16)
    own_grad = jnp.concatenate(
        [
            grad_query.reshape(rows, width),
            grad_keyed.reshape(rows, width),
            grad_valued.reshape(rows, width),
        ],
        axis=1,
    )
    grad_query_b = jnp.sum(own_grad[:, :width].astype(jnp.float32), axis=0)
    grad_value_b = jnp.sum(own_grad[:, 2 * width :].astype(jnp.float32), axis=0)
    grad_qkv_w = inner(inputs, own_grad).astype(jnp.bfloat16)
    grad_inputs = (grad_resid + times_transposed(own_grad, whole_qkv)).astype(jnp.bfloat16)
    group_in = lax.all_gather(grad_inputs, "ctx", axis=0, tiled=True)
    in_home = jnp.dot(home, group_in, preferred_element_type=jnp.float32)

    def summed(grad):
        part = lax.psum_scatter(grad, "wsh", scatter_dimension=0, tiled=True)
        return lax.psum(part, "ctx").astype(jnp.float32)

    sums = [summed(g) for g in (grad_down_w, grad_up_w, grad_out_w, grad_qkv_w)]
    small_grads = [
        grad_query_b,
        grad_value_b,
        grad_out_b,
        grad_gain_one,
        grad_shift_one,
        grad_down_b,
        grad_gain_two,
        grad_shift_two,
        grad_up_b,
    ]
    parts = lax.axis_size("wsh")
    table = jnp.concatenate([g.reshape(parts, -1) for g in small_grads], axis=1)
    table = lax.psum(table, ("ctx", "wsh"))
    own = lax.dynamic_slice_in_dim(table, lax.axis_index("wsh"), 1, 0)[0]
    g_q, g_v, g_o, g_g1, g_s1, g_d, g_g2, g_s2, g_u = [own[s : s + n] for s, n in zip(spots, sizes)]
    return (
        out_home[None],
        in_home[None],
        sums[3],
        g_q,
        g_v,
        sums[2],
        g_o,
        g_g1,
        g_s1,
        sums[1],
        g_u,
        sums[0],
        g_d,
        g_g2,
        g_s2,
    )


def solution(mesh):
    row = P("wsh", None)
    vec = P("wsh")
    seq = P("wsh", "ctx", None)
    in_specs = (
        seq,
        P("wsh", "ctx"),
        row,
        vec,
        vec,
        row,
        vec,
        vec,
        vec,
        row,
        vec,
        row,
        vec,
        vec,
        vec,
        seq,
    )
    out_specs = (seq, seq, row, vec, vec, row, vec, vec, vec, row, vec, row, vec, vec, vec)
    return jax.shard_map(
        on_device, mesh=mesh, in_specs=in_specs, out_specs=out_specs, check_vma=False
    )
```

profile of v0, /device:TPU:0, one launch (start us, length us, event | category | flops | bytes accessed | tf_op | source)
XLA Modules:
  0.0 654.2 jit_solution(16202312041115670555)
XLA Ops:
  7.2 2.6 pad_maximum_fusion
  10.0 0.7 all-gather.13.cloned.1.call-update
  10.8 0.7 all-gather.15.cloned.1.call-update
  12.1 0.5 all-gather.19.cloned.1.call-update
  12.8 15.7 %all-gather.2 = bf16[8,1,1152]{2,1,0:T(2,128)(2,1)S(1)} all-gather(bf16[1,1,1152]{2,1,0:T(2,128)(2,1)S(1)} %reshape.237), channel_id=3, replica_groups=mesh['ctx'=4,'wsh'=8] {'wsh'}, dimensions={0}, use_global_device_ids=true | all-gather | bytes 20736 | tf_op jit(solution)/shard_map/all_gather | solution.py:76
  29.4 53.9 %all-gather.11.cloned.1.call-done = bf16[2048,1536]{1,0:T(8,128)(2,1)} async-done(((bf16[512,1536]{1,0:T(8,128)(2,1)}), bf16[2048,1536]{1,0:T(8,128)(2,1)}) %all-gather.11.cloned.1.call-update) | async-done | bytes 6291472 | tf_op jit(solution)/shard_map/all_gather | solution.py:82
  83.3 5.8 fusion.12
  89.2 37.4 %all-gather.13.cloned.1.call-done = bf16[768,2304]{1,0:T(8,128)(2,1)} async-done(((bf16[96,2304]{1,0:T(8,128)(2,1)}), bf16[768,2304]{1,0:T(8,128)(2,1)}) %all-gather.13.cloned.1.call-update) | async-done | bytes 3538960 | tf_op jit(solution)/shard_map/all_gather | solution.py:85
  126.5 4.0 fusion.11
  130.5 1.4 fusion.67
  132.0 1.5 copy.64
  135.1 0.6 fusion.52
  135.7 1.0 fusion.68
  136.8 0.6 fusion.35
  137.4 1.0 copy-done.11
  138.4 0.6 copy.70
  139.0 10.7 %all-gather.15.cloned.1.call-done = bf16[768,768]{1,0:T(8,128)(2,1)} async-done(((bf16[96,768]{1,0:T(8,128)(2,1)}), bf16[768,768]{1,0:T(8,128)(2,1)}) %all-gather.15.cloned.1.call-update) | async-done | bytes 1179664 | tf_op jit(solution)/shard_map/all_gather | solution.py:86
  149.7 2.7 fusion.26
  152.4 2.1 multiply_reduce_fusion.6
  154.5 48.2 %all-gather.17.cloned.1.call-done = bf16[768,3072]{1,0:T(8,128)(2,1)} async-done(((bf16[96,3072]{1,0:T(8,128)(2,1)}), bf16[768,3072]{1,0:T(8,128)(2,1)}) %all-gather.17.cloned.1.call-update) | async-done | bytes 4718608 | tf_op jit(solution)/shard_map/all_gather | solution.py:87
  202.7 9.0 %multiply_convert_fusion = (bf16[512,3072]{1,0:T(8,128)(2,1)}, f32[512,3072]{1,0:T(8,128)}) fusion(f32[3072]{0:T(1024)S(1)} %reshape.231, bf16[768,3072]{1,0:T(8,128)(2,1)} %all-gather.17.cloned.1.call-done, f32[768]{0:T(1024)S(1)} %reshape.230, f32[768]{0:T(1024)S(1)} %reshape.229, f32[512]{0:T(512)S(1)} %add_rsqrt_fusion.1, ...), kind=kOutput, calls=%fused_computation.9 | convolution fusion | flops 2428502016 | bytes 15751168 | tf_op jit(solution)/shard_map/dot_general | solution.py:128
  211.8 43.0 %all-gather.19.cloned.1.call-done = bf16[3072,768]{1,0:T(8,128)(2,1)} async-done(((bf16[384,768]{1,0:T(8,128)(2,1)}), bf16[3072,768]{1,0:T(8,128)(2,1)}) %all-gather.19.cloned.1.call-update) | async-done | bytes 4718608 | tf_op jit(solution)/shard_map/all_gather | solution.py:88
  254.8 6.7 %fusion.69 = (f32[512]{0:T(512)S(1)}, f32[512,768]{1,0:T(8,128)S(1)}) fusion(f32[768]{0:T(1024)S(1)} %reshape.232, bf16[512,3072]{1,0:T(8,128)(2,1)} %get-tuple-element.55, bf16[3072,768]{1,0:T(8,128)(2,1)} %all-gather.19.cloned.1.call-done, f32[768]{0:T(1024)S(1)} %reshape.230, f32[768]{0:T(1024)S(1)} %reshape.229, f32[512]{0:T(512)S(1)} %add_rsqrt_fusion.1, ...), kind=kOutput, calls=%fused_computation.137 | convolution fusion | flops 2419850752 | bytes 11025408 | tf_op jit(solution)/shard_map/dot_general | solution.py:132
  261.8 0.8 multiply_reduce_fusion.1
  262.7 1.5 convert_reduce_fusion.1
  264.2 4.7 convert_reduce_fusion
  269.0 3.2 multiply_reduce_fusion.2
  272.3 1.9 convert_reduce_fusion.2
  274.1 1.7 convolution_convert_fusion.4
  275.9 2.3 copy.71
  278.2 2.6 reshape.213
  280.8 4.4 convert_reduce_fusion.3
  285.2 2.5 multiply_reduce_fusion
  287.7 1.8 convolution_convert_fusion.3
  289.5 2.6 copy.82
  292.2 3.8 multiply_convert_fusion.1
  295.9 1.2 fusion.38
  297.1 0.6 copy.79
  297.8 0.7 convert_reduce_fusion.4
  298.4 0.6 copy.76
  299.7 1.4 copy-done.19
  301.1 0.7 copy-done.2
  301.8 3.9 convolution_convert_fusion.2
  305.8 7.2 %convolution_convert_fusion.1 = bf16[768,3072]{1,0:T(8,128)(2,1)} fusion(bf16[512,3072]{1,0:T(8,128)(2,1)} %copy-done.34, f32[768]{0:T(1024)S(1)} %reshape.230, f32[768]{0:T(1024)S(1)} %reshape.229, bf16[512,768]{1,0:T(8,128)(2,1)} %copy-done.5, f32[512]{0:T(512)S(1)} %add_rsqrt_fusion.1, f32[512]{0:T(512)S(1)} %broadcast_multiply_fusion.5, ...), kind=kOutput, calls=%fused_computation.16 | convolution fusion | flops 2421424128 | bytes 9449472 | tf_op jit(solution)/shard_map/dot_general | solution.py:12
  313.2 1.1 copy-done.14
  314.3 6.7 %convolution_convert_fusion = bf16[3072,768]{1,0:T(8,128)(2,1)} fusion(bf16[512,3072]{1,0:T(8,128)(2,1)} %get-tuple-element.55, f32[512,768]{1,0:T(8,128)S(1)} %copy-done.14), kind=kOutput, calls=%fused_computation.15 | convolution fusion | flops 2418671616 | bytes 9437184 | tf_op jit(solution)/shard_map/dot_general | solution.py:12
  321.1 1.3 copy-done.4
  322.5 5.7 add_convert_fusion
  328.2 0.7 all-gather.21.cloned.1.call-update
  329.0 39.3 %reduce-scatter.5.cloned.1.call-done = bf16[96,2304]{1,0:T(8,128)(2,1)} async-done(((bf16[768,2304]{1,0:T(8,128)(2,1)}), bf16[96,2304]{1,0:T(8,128)(2,1)}) %reduce-scatter.5.cloned.1.call-update) | async-done | bytes 442384 | tf_op jit(solution)/shard_map/reduce_scatter | solution.py:191
  368.3 55.9 %reduce-scatter.9.cloned.1.call-done = bf16[96,3072]{1,0:T(8,128)(2,1)} async-done(((bf16[768,3072]{1,0:T(8,128)(2,1)}), bf16[96,3072]{1,0:T(8,128)(2,1)}) %reduce-scatter.9.cloned.1.call-update) | async-done | bytes 589840 | tf_op jit(solution)/shard_map/reduce_scatter | solution.py:191
  424.2 55.8 %reduce-scatter.11.cloned.1.call-done = bf16[384,768]{1,0:T(8,128)(2,1)} async-done(((bf16[3072,768]{1,0:T(8,128)(2,1)}), bf16[384,768]{1,0:T(8,128)(2,1)}) %reduce-scatter.11.cloned.1.call-update) | async-done | bytes 589840 | tf_op jit(solution)/shard_map/reduce_scatter | solution.py:191
  480.0 8.0 %all-gather = s32[1,2048]{1,0:T(1,128)S(1)} all-gather(s32[1,512]{1,0:T(1,128)S(1)} %copy-done.21), channel_id=2, replica_groups=mesh['ctx'=4,'wsh'=8] {'ctx'}, dimensions={1}, use_global_device_ids=true | all-gather | bytes 10240 | tf_op jit(solution)/shard_map/all_gather | solution.py:81
  488.7 37.6 %psum.36 = f32[8,1152]{1,0:T(8,128)S(1)} all-reduce(f32[8,1152]{1,0:T(8,128)S(1)} %concatenate.19), channel_id=1, replica_groups=mesh['ctx'=4,'wsh'=8] {'ctx','wsh'}, use_global_device_ids=true, to_apply=%region_22.23 | all-reduce | flops 9216 | bytes 73728 | tf_op jit(solution)/shard_map/psum | solution.py:208
  526.2 0.7 dynamic-slice_reduce_fusion
  526.9 0.6 dynamic-slice_bitcast_fusion
  527.5 4.9 fusion.22
  532.4 40.1 %all-gather.21.cloned.1.call-done = bf16[2048,768]{1,0:T(8,128)(2,1)} async-done(((bf16[512,768]{1,0:T(8,128)(2,1)}), bf16[2048,768]{1,0:T(8,128)(2,1)}) %all-gather.21.cloned.1.call-update) | async-done | bytes 3145744 | tf_op jit(solution)/shard_map/all_gather | solution.py:135
  572.5 4.6 fusion.32
  577.1 63.9 %all-reduce.3.cloned.1.call-done = (bf16[96,2304]{1,0:T(8,128)(2,1)}, bf16[96,768]{1,0:T(8,128)(2,1)}, bf16[96,3072]{1,0:T(8,128)(2,1)}, bf16[384,768]{1,0:T(8,128)(2,1)}) async-done(((bf16[96,2304]{1,0:T(8,128)(2,1)}, bf16[96,768]{1,0:T(8,128)(2,1)}, bf16[96,3072]{1,0:T(8,128)(2,1)}, bf16[384,768]{1,0:T(8,128)(2,1)}), (bf16[96,2304]{1,0:T(8,128)(2,1)}, bf16[96,768]{1,0:T(8,128)(2,1)}, ...) | async-done | bytes 1769488 | tf_op jit(solution)/shard_map/psum | solution.py:192
  641.0 2.2 convert_element_type.246
  643.3 2.2 convert_element_type.248
  645.4 1.0 convert_element_type.237
  646.4 0.7 convert_element_type.244
  (136 shorter events, 5.6 us)
Async XLA Ops:
  7.2 76.1 %all-gather.11.cloned.1.call-start = ((), (), s32[]{:S(2)}) async-start(), calls=%async_computation.4 | async-start | bytes 7864320 | tf_op jit(solution)/shard_map/all_gather | solution.py:82
  9.8 2.8 copy-start.22
  9.8 2.8 copy-start.23
  9.9 2.8 copy-start.24
  9.9 2.8 copy-start.25
  9.9 2.8 copy-start.26
  9.9 2.8 copy-start.27
  9.9 2.8 copy-start.28
  9.9 2.8 copy-start.29
  9.9 2.8 copy-start.30
  9.9 19.3 %copy-start.21 = (s32[1,512]{1,0:T(1,128)S(1)}, s32[1,512]{1,0:T(1,128)}, u32[]{:S(2)}) copy-start(s32[1,512]{1,0:T(1,128)} %param.17) | copy-start | bytes 6148
  10.0 116.6 %all-gather.13.cloned.1.call-start = ((), (), s32[]{:S(2)}) async-start(), calls=%async_computation.5 | async-start | bytes 3981312 | tf_op jit(solution)/shard_map/all_gather | solution.py:85
  10.7 139.0 %all-gather.15.cloned.1.call-start = ((), (), s32[]{:S(2)}) async-start(), calls=%async_computation.6 | async-start | bytes 1327104 | tf_op jit(solution)/shard_map/all_gather | solution.py:86
  11.4 191.3 %all-gather.17.cloned.1.call-start = ((), (), s32[]{:S(2)}) async-start(), calls=%async_computation.7 | async-start | bytes 5308416 | tf_op jit(solution)/shard_map/all_gather | solution.py:87
  12.0 242.8 %all-gather.19.cloned.1.call-start = ((), (), s32[]{:S(2)}) async-start(), calls=%async_computation.8 | async-start | bytes 5308416 | tf_op jit(solution)/shard_map/all_gather | solution.py:88
  12.6 316.4 %reduce-scatter.7.cloned.1.call-start = ((), (), s32[]{:S(2)}) async-start(), calls=%async_computation.12 | async-start | bytes 1327104 | tf_op jit(solution)/shard_map/reduce_scatter | solution.py:191
  89.2 41.4 %copy-start = (f32[512,1536]{1,0:T(8,128)}, f32[512,1536]{1,0:T(8,128)S(1)}, u32[]{:S(2)}) copy-start(f32[512,1536]{1,0:T(8,128)S(1)} %fusion.12) | copy-start | bytes 9437188
  132.0 1.7 copy-start.9
  133.5 1.2 copy-start.8
  135.1 1.7 copy-start.15
  136.8 1.6 copy-start.11
  139.0 13.4 %copy-start.6 = (bf16[4,128,12,64]{1,0,3,2:T(4,128)(2,1)}, bf16[4,128,12,64]{1,0,3,2:T(4,128)(2,1)S(1)}, u32[]{:S(2)}) copy-start(bf16[4,128,12,64]{1,0,3,2:T(4,128)(2,1)S(1)} %copy.70) | copy-start | bytes 2359300
  152.4 116.5 %copy-start.5 = (bf16[512,768]{1,0:T(8,128)(2,1)}, bf16[512,768]{1,0:T(8,128)(2,1)S(1)}, u32[]{:S(2)}) copy-start(bf16[512,768]{1,0:T(8,128)(2,1)S(1)} %get-tuple-element.54) | copy-start | bytes 2359300
  254.8 7.0 %copy-start.1 = (f32[512,1536]{1,0:T(8,128)S(1)}, f32[512,1536]{1,0:T(8,128)}, u32[]{:S(2)}) copy-start(f32[512,1536]{1,0:T(8,128)} %copy-done) | copy-start | bytes 9437188
  254.8 9.4 %copy-start.33 = (f32[512,3072]{1,0:T(8,128)S(1)}, f32[512,3072]{1,0:T(8,128)}, u32[]{:S(2)}) copy-start(f32[512,3072]{1,0:T(8,128)} %get-tuple-element.56) | copy-start | bytes 18874372
  261.8 2.4 copy-start.31
  262.6 6.3 slice-start
  264.2 4.8 copy-start.13
  264.2 4.8 slice-start.1
  268.9 3.3 copy-start.34
  272.2 1.9 copy-start.32
  274.1 13.5 %copy-start.3 = (f32[512,768]{1,0:T(8,128)}, f32[512,768]{1,0:T(8,128)S(1)}, u32[]{:S(2)}) copy-start(f32[512,768]{1,0:T(8,128)S(1)} %get-tuple-element.30) | copy-start | bytes 4718596
  280.8 4.4 copy-start.12
  280.8 4.4 copy-start.16
  280.8 4.4 copy-start.17
  285.2 2.5 copy-start.7
  292.1 76.1 %reduce-scatter.5.cloned.1.call-start = ((), (), s32[]{:S(2)}) async-start(), calls=%async_computation.11 | async-start | bytes 3981312 | tf_op jit(solution)/shard_map/reduce_scatter | solution.py:191
  298.4 1.1 copy-start.10
  299.1 2.7 copy-start.2
  299.7 1.4 copy-start.19
  305.7 118.5 %reduce-scatter.9.cloned.1.call-start = ((), (), s32[]{:S(2)}) async-start(), calls=%async_computation.13 | async-start | bytes 5308416 | tf_op jit(solution)/shard_map/reduce_scatter | solution.py:191
  312.9 1.4 copy-start.14
  313.0 167.0 %reduce-scatter.11.cloned.1.call-start = ((), (), s32[]{:S(2)}) async-start(), calls=%async_computation.14 | async-start | bytes 5308416 | tf_op jit(solution)/shard_map/reduce_scatter | solution.py:191
  321.1 1.4 copy-start.4
  321.1 206.4 %all-gather.23.cloned.1.call-start = ((), (), s32[]{:S(2)}) async-start(), calls=%async_computation.10 | async-start | bytes 3932160 | tf_op jit(solution)/shard_map/all_gather | solution.py:187
  328.2 244.4 %all-gather.21.cloned.1.call-start = ((), (), s32[]{:S(2)}) async-start(), calls=%async_computation.9 | async-start | bytes 3932160 | tf_op jit(solution)/shard_map/all_gather | solution.py:135
  328.9 312.1 %all-reduce.3.cloned.1.call-start = ((), (), s32[]{:S(2)}) async-start(), calls=%async_computation.15 | async-start | bytes 3538944 | tf_op jit(solution)/shard_map/psum | solution.py:192
  641.0 4.4 copy-start.18
  641.0 5.4 copy-start.20
Sparse Core Ops, SparseCore 0:
  10.4 72.8 all-gather.10
  85.0 41.5 all-gather.12
  128.2 21.5 all-gather.14
  151.2 51.4 all-gather.16
  204.2 50.5 all-gather.18
  292.2 31.5 reduce-scatter.6
  326.2 42.0 reduce-scatter.4
  370.7 53.4 reduce-scatter.8
  426.6 53.3 reduce-scatter.10
  482.3 43.4 all-gather.22
  528.4 44.0 all-gather.20
  576.2 64.7 all-reduce.2
where the time goes:
time: 663 us; the launch traced here: 654 us
  waiting for transfers between devices  451 us (68%)
  matrix products  82.5 us (12%)
  blocking collectives  61.3 us (9%)
  local copies, waits for them, and re-layouts  22.8 us (3%)
  other arithmetic  20.3 us (3%)
  between operations  15.1 us (2%)
    reduce_scatter x4, waiting for transfers between devices, summed(): part = lax.psum_scatter(grad, 'wsh', scatter_dimension=0, tiled=True)  151 us
    psum x1, waiting for transfers between devices, summed(): return lax.psum(part, 'ctx').astype(jnp.float32)  63.9 us
    all_gather x1, waiting for transfers between devices, on_device(): lax.all_gather(jnp.concatenate([tokens[0], cotangent[0]], axis=1), 'ctx',...  53.9 us
    all_gather x1, waiting for transfers between devices, on_device(): whole_up = lax.all_gather(up_weight, 'wsh', axis=0, tiled=True)  48.2 us
    all_gather x1, waiting for transfers between devices, on_device(): whole_down = lax.all_gather(down_weight, 'wsh', axis=0, tiled=True)  43 us
    all_gather x1, waiting for transfers between devices, on_device(): group_out = lax.all_gather(layer_out, 'ctx', axis=0, tiled=True)  40.1 us
    psum x1, blocking collectives, on_device(): table = lax.psum(table, ('ctx', 'wsh'))  37.6 us
    all_gather x1, waiting for transfers between devices, on_device(): whole_qkv = lax.all_gather(qkv_weight, 'wsh', axis=0, tiled=True)  37.4 us
  transfers between devices with their start and end apart: 12, of which 10 were waited for; matrix products, arithmetic and copies ran while one was open for 11% of the time, Pallas kernels for 0%

commit v1 on v0

--- a/solution.py
+++ b/solution.py
@@ -189,7 +189,7 @@
 
     def summed(grad):
         part = lax.psum_scatter(grad, "wsh", scatter_dimension=0, tiled=True)
-        return lax.psum(part, "ctx").astype(jnp.float32)
+        return jnp.sum(lax.all_gather(part, "ctx"), axis=0).astype(jnp.float32)
 
     sums = [summed(g) for g in (grad_down_w, grad_up_w, grad_out_w, grad_qkv_w)]
     small_grads = [

time: 663 us -> 706 us (1.065)
  waiting for transfers between devices: 451 us -> 479 us
  blocking collectives: 61.3 us -> 73.9 us
  matrix products: 82.5 us -> 90.1 us
    all_gather x0 -> x3, waiting for transfers between devices: none -> 103 us  [summed(): return jnp.sum(lax.all_gather(part, 'ctx'), axis=0).astype(jnp.float32)]
    psum x1 -> x0, waiting for transfers between devices: 63.9 us -> none  [summed(): return lax.psum(part, 'ctx').astype(jnp.float32)]
    reduce_scatter x4, waiting for transfers between devices: 151 us -> 129 us  [summed(): part = lax.psum_scatter(grad, 'wsh', scatter_dimension=0, tiled=True)]
    all_gather x1, waiting for transfers between devices: 0.01 us -> 19.8 us  [on_device(): group_in = lax.all_gather(grad_inputs, 'ctx', axis=0, tiled=True)]
    all_gather x0 -> x1, blocking collectives: none -> 12.7 us  [summed(): return jnp.sum(lax.all_gather(part, 'ctx'), axis=0).astype(jnp.float32)]
    dot_general x1, matrix products: 9.02 us -> 20 us  [on_device(): jnp.dot(first_low, whole_up, preferred_element_type=jnp.float32) + ubias]
    all_gather x1, waiting for transfers between devices: 43 us -> 32 us  [on_device(): whole_down = lax.all_gather(down_weight, 'wsh', axis=0, tiled=True)]
  transfers between devices with their start and end apart: 12 -> 14, of which waited for: 10 -> 13; matrix products, arithmetic and copies ran while one was open for 11% -> 12% of each run, Pallas kernels for 0% -> 0%
where the time goes in v1:
time: 706 us; the launch traced here: 697 us
  waiting for transfers between devices  479 us (68%)
  matrix products  90.1 us (13%)
  blocking collectives  73.9 us (10%)
  other arithmetic  20.4 us (3%)
  local copies, waits for them, and re-layouts  18 us (3%)
  between operations  15 us (2%)
    reduce_scatter x4, waiting for transfers between devices, summed(): part = lax.psum_scatter(grad, 'wsh', scatter_dimension=0, tiled=True)  129 us
    all_gather x3, waiting for transfers between devices, summed(): return jnp.sum(lax.all_gather(part, 'ctx'), axis=0).astype(jnp.float32)  103 us
    all_gather x1, waiting for transfers between devices, on_device(): lax.all_gather(jnp.concatenate([tokens[0], cotangent[0]], axis=1), 'ctx',...  53.9 us
    all_gather x1, waiting for transfers between devices, on_device(): whole_up = lax.all_gather(up_weight, 'wsh', axis=0, tiled=True)  48.2 us
    all_gather x1, waiting for transfers between devices, on_device(): group_out = lax.all_gather(layer_out, 'ctx', axis=0, tiled=True)  41.7 us
    psum x1, blocking collectives, on_device(): table = lax.psum(table, ('ctx', 'wsh'))  37.5 us
    all_gather x1, waiting for transfers between devices, on_device(): whole_qkv = lax.all_gather(qkv_weight, 'wsh', axis=0, tiled=True)  37.4 us
    all_gather x1, waiting for transfers between devices, on_device(): whole_down = lax.all_gather(down_weight, 'wsh', axis=0, tiled=True)  32 us
  transfers between devices with their start and end apart: 14, of which 13 were waited for; matrix products, arithmetic and copies ran while one was open for 12% of the time, Pallas kernels for 0%

profile of v1, /device:TPU:0, one launch (start us, length us, event | category | flops | bytes accessed | tf_op | source)
XLA Modules:
  0.0 696.8 jit_solution(15674654837465826455)
XLA Ops:
  7.2 2.6 pad_maximum_fusion
  10.0 0.7 all-gather.20.cloned.1.call-update
  10.8 0.7 all-gather.22.cloned.1.call-update
  12.8 15.7 %all-gather.6 = bf16[8,1,1152]{2,1,0:T(2,128)(2,1)S(1)} all-gather(bf16[1,1,1152]{2,1,0:T(2,128)(2,1)S(1)} %reshape.241), channel_id=3, replica_groups=mesh['ctx'=4,'wsh'=8] {'wsh'}, dimensions={0}, use_global_device_ids=true | all-gather | bytes 20736 | tf_op jit(solution)/shard_map/all_gather | solution.py:76
  29.4 53.9 %all-gather.18.cloned.1.call-done = bf16[2048,1536]{1,0:T(8,128)(2,1)} async-done(((bf16[512,1536]{1,0:T(8,128)(2,1)}), bf16[2048,1536]{1,0:T(8,128)(2,1)}) %all-gather.18.cloned.1.call-update) | async-done | bytes 6291472 | tf_op jit(solution)/shard_map/all_gather | solution.py:82
  83.3 5.8 fusion.12
  89.2 37.4 %all-gather.20.cloned.1.call-done = bf16[768,2304]{1,0:T(8,128)(2,1)} async-done(((bf16[96,2304]{1,0:T(8,128)(2,1)}), bf16[768,2304]{1,0:T(8,128)(2,1)}) %all-gather.20.cloned.1.call-update) | async-done | bytes 3538960 | tf_op jit(solution)/shard_map/all_gather | solution.py:85
  126.5 4.0 fusion.11
  130.5 1.4 fusion.67
  132.0 1.5 copy.64
  135.1 0.6 fusion.52
  135.7 1.0 fusion.68
  137.4 1.1 copy-done.10
  139.1 10.7 %all-gather.22.cloned.1.call-done = bf16[768,768]{1,0:T(8,128)(2,1)} async-done(((bf16[96,768]{1,0:T(8,128)(2,1)}), bf16[768,768]{1,0:T(8,128)(2,1)}) %all-gather.22.cloned.1.call-update) | async-done | bytes 1179664 | tf_op jit(solution)/shard_map/all_gather | solution.py:86
  149.7 2.7 fusion.26
  152.4 2.1 multiply_reduce_fusion.6
  154.5 48.2 %all-gather.24.cloned.1.call-done = bf16[768,3072]{1,0:T(8,128)(2,1)} async-done(((bf16[96,3072]{1,0:T(8,128)(2,1)}), bf16[768,3072]{1,0:T(8,128)(2,1)}) %all-gather.24.cloned.1.call-update) | async-done | bytes 4718608 | tf_op jit(solution)/shard_map/all_gather | solution.py:87
  202.8 20.0 %multiply_convert_fusion = (bf16[512,3072]{1,0:T(8,128)(2,1)}, f32[512,3072]{1,0:T(8,128)}) fusion(f32[3072]{0:T(1024)S(1)} %reshape.231, bf16[768,3072]{1,0:T(8,128)(2,1)} %all-gather.24.cloned.1.call-done, f32[768]{0:T(1024)S(1)} %reshape.230, f32[768]{0:T(1024)S(1)} %reshape.229, f32[512]{0:T(512)S(1)} %add_rsqrt_fusion.1, ...), kind=kOutput, calls=%fused_computation.9 | convolution fusion | flops 2428502016 | bytes 15751168 | tf_op jit(solution)/shard_map/dot_general | solution.py:128
  222.8 32.0 %all-gather.26.cloned.1.call-done = bf16[3072,768]{1,0:T(8,128)(2,1)} async-done(((bf16[384,768]{1,0:T(8,128)(2,1)}), bf16[3072,768]{1,0:T(8,128)(2,1)}) %all-gather.26.cloned.1.call-update) | async-done | bytes 4718608 | tf_op jit(solution)/shard_map/all_gather | solution.py:88
  254.8 6.7 fusion.69
  261.8 0.8 multiply_reduce_fusion.1
  262.7 1.5 convert_reduce_fusion.1
  264.2 4.7 convert_reduce_fusion
  269.0 3.2 multiply_reduce_fusion.2
  272.9 1.1 copy-done.3
  274.0 0.8 convolution_convert_fusion.4
  275.4 3.3 convert_reduce_fusion.3
  278.7 0.9 multiply_reduce_fusion
  279.6 1.0 multiply_convert_fusion.1
  280.6 0.7 convert_reduce_fusion.4
  281.3 1.2 fusion.38
  283.1 0.6 copy.79
  283.7 0.6 copy.76
  284.7 1.4 copy-done.16
  286.1 1.0 copy-done.2
  287.1 4.1 convolution_convert_fusion.2
  291.2 7.2 %convolution_convert_fusion.1 = bf16[768,3072]{1,0:T(8,128)(2,1)} fusion(bf16[512,3072]{1,0:T(8,128)(2,1)} %copy-done.30, f32[768]{0:T(1024)S(1)} %reshape.230, f32[768]{0:T(1024)S(1)} %reshape.229, bf16[512,768]{1,0:T(8,128)(2,1)} %copy-done.7, f32[512]{0:T(512)S(1)} %add_rsqrt_fusion.1, f32[512]{0:T(512)S(1)} %broadcast_multiply_fusion.5, ...), kind=kOutput, calls=%fused_computation.16 | convolution fusion | flops 2421424128 | bytes 9449472 | tf_op jit(solution)/shard_map/dot_general | solution.py:12
  298.5 1.3 copy-done.13
  299.8 6.7 convolution_convert_fusion
  306.6 1.3 copy-done.4
  308.1 1.8 convolution_convert_fusion.3
  310.0 5.7 add_convert_fusion
  315.7 0.7 all-gather.28.cloned.1.call-update
  316.5 17.5 %reduce-scatter.5.cloned.1.call-done = bf16[96,2304]{1,0:T(8,128)(2,1)} async-done(((bf16[768,2304]{1,0:T(8,128)(2,1)}), bf16[96,2304]{1,0:T(8,128)(2,1)}) %reduce-scatter.5.cloned.1.call-update) | async-done | bytes 442384 | tf_op jit(solution)/shard_map/reduce_scatter | solution.py:191
  334.0 55.9 %reduce-scatter.9.cloned.1.call-done = bf16[96,3072]{1,0:T(8,128)(2,1)} async-done(((bf16[768,3072]{1,0:T(8,128)(2,1)}), bf16[96,3072]{1,0:T(8,128)(2,1)}) %reduce-scatter.9.cloned.1.call-update) | async-done | bytes 589840 | tf_op jit(solution)/shard_map/reduce_scatter | solution.py:191
  389.9 55.7 %reduce-scatter.11.cloned.1.call-done = bf16[384,768]{1,0:T(8,128)(2,1)} async-done(((bf16[3072,768]{1,0:T(8,128)(2,1)}), bf16[384,768]{1,0:T(8,128)(2,1)}) %reduce-scatter.11.cloned.1.call-update) | async-done | bytes 589840 | tf_op jit(solution)/shard_map/reduce_scatter | solution.py:191
  445.7 8.0 %all-gather = s32[1,2048]{1,0:T(1,128)S(1)} all-gather(s32[1,512]{1,0:T(1,128)S(1)} %copy-done.17), channel_id=2, replica_groups=mesh['ctx'=4,'wsh'=8] {'ctx'}, dimensions={1}, use_global_device_ids=true | all-gather | bytes 10240 | tf_op jit(solution)/shard_map/all_gather | solution.py:81
  454.4 37.5 %psum.7 = f32[8,1152]{1,0:T(8,128)S(1)} all-reduce(f32[8,1152]{1,0:T(8,128)S(1)} %concatenate.19), channel_id=1, replica_groups=mesh['ctx'=4,'wsh'=8] {'ctx','wsh'}, use_global_device_ids=true, to_apply=%region_22.23 | all-reduce | flops 9216 | bytes 73728 | tf_op jit(solution)/shard_map/psum | solution.py:208
  491.9 0.7 dynamic-slice_reduce_fusion
  493.2 12.7 %all-gather.3 = bf16[384,768]{1,0:T(8,128)(2,1)S(1)} all-gather(bf16[96,768]{1,0:T(8,128)(2,1)} %reduce-scatter.7.cloned.1.call-done), channel_id=5, replica_groups=mesh['ctx'=4,'wsh'=8] {'ctx'}, dimensions={0}, use_global_device_ids=true | all-gather | bytes 737280 | tf_op jit(solution)/shard_map/all_gather | solution.py:192
  506.0 0.7 convert_element_type.252
  506.7 19.8 %all-gather.30.cloned.1.call-done = bf16[2048,768]{1,0:T(8,128)(2,1)} async-done(((bf16[512,768]{1,0:T(8,128)(2,1)}), bf16[2048,768]{1,0:T(8,128)(2,1)}) %all-gather.30.cloned.1.call-update) | async-done | bytes 3145744 | tf_op jit(solution)/shard_map/all_gather | solution.py:187
  526.5 4.9 fusion.22
  531.4 41.7 %all-gather.28.cloned.1.call-done = bf16[2048,768]{1,0:T(8,128)(2,1)} async-done(((bf16[512,768]{1,0:T(8,128)(2,1)}), bf16[2048,768]{1,0:T(8,128)(2,1)}) %all-gather.28.cloned.1.call-update) | async-done | bytes 3145744 | tf_op jit(solution)/shard_map/all_gather | solution.py:135
  573.1 4.6 fusion.32
  577.7 29.9 %all-gather.32.cloned.1.call-done = bf16[384,2304]{1,0:T(8,128)(2,1)} async-done(((bf16[96,2304]{1,0:T(8,128)(2,1)}), bf16[384,2304]{1,0:T(8,128)(2,1)}) %all-gather.32.cloned.1.call-update) | async-done | bytes 1769488 | tf_op jit(solution)/shard_map/all_gather | solution.py:192
  607.6 1.8 reduce_sum.229
  609.3 1.0 convert_element_type.245
  610.3 36.7 %all-gather.34.cloned.1.call-done = bf16[384,3072]{1,0:T(8,128)(2,1)} async-done(((bf16[96,3072]{1,0:T(8,128)(2,1)}), bf16[384,3072]{1,0:T(8,128)(2,1)}) %all-gather.34.cloned.1.call-update) | async-done | bytes 2359312 | tf_op jit(solution)/shard_map/all_gather | solution.py:192
  647.1 2.1 reduce_sum.240
  649.2 1.1 convert_element_type.254
  650.3 36.1 %all-gather.36.cloned.1.call-done = bf16[1536,768]{1,0:T(8,128)(2,1)} async-done(((bf16[384,768]{1,0:T(8,128)(2,1)}), bf16[1536,768]{1,0:T(8,128)(2,1)}) %all-gather.36.cloned.1.call-update) | async-done | bytes 2359312 | tf_op jit(solution)/shard_map/all_gather | solution.py:192
  686.4 2.3 reduce_sum.241
  688.7 1.1 convert_element_type.256
  (139 shorter events, 9.5 us)
Async XLA Ops:
  7.2 76.1 %all-gather.18.cloned.1.call-start = ((), (), s32[]{:S(2)}) async-start(), calls=%async_computation.4 | async-start | bytes 7864320 | tf_op jit(solution)/shard_map/all_gather | solution.py:82
  9.8 2.8 copy-start.18
  9.9 2.8 copy-start.19
  9.9 2.8 copy-start.20
  9.9 2.8 copy-start.21
  9.9 2.8 copy-start.22
  9.9 2.8 copy-start.23
  9.9 2.8 copy-start.24
  9.9 2.8 copy-start.25
  9.9 2.8 copy-start.26
  9.9 19.3 %copy-start.17 = (s32[1,512]{1,0:T(1,128)S(1)}, s32[1,512]{1,0:T(1,128)}, u32[]{:S(2)}) copy-start(s32[1,512]{1,0:T(1,128)} %param.17) | copy-start | bytes 6148
  10.0 116.6 %all-gather.20.cloned.1.call-start = ((), (), s32[]{:S(2)}) async-start(), calls=%async_computation.5 | async-start | bytes 3981312 | tf_op jit(solution)/shard_map/all_gather | solution.py:85
  10.7 139.0 %all-gather.22.cloned.1.call-start = ((), (), s32[]{:S(2)}) async-start(), calls=%async_computation.6 | async-start | bytes 1327104 | tf_op jit(solution)/shard_map/all_gather | solution.py:86
  11.4 191.3 %all-gather.24.cloned.1.call-start = ((), (), s32[]{:S(2)}) async-start(), calls=%async_computation.7 | async-start | bytes 5308416 | tf_op jit(solution)/shard_map/all_gather | solution.py:87
  12.0 242.8 %all-gather.26.cloned.1.call-start = ((), (), s32[]{:S(2)}) async-start(), calls=%async_computation.8 | async-start | bytes 5308416 | tf_op jit(solution)/shard_map/all_gather | solution.py:88
  12.6 321.3 %reduce-scatter.5.cloned.1.call-start = ((), (), s32[]{:S(2)}) async-start(), calls=%async_computation.11 | async-start | bytes 3981312 | tf_op jit(solution)/shard_map/reduce_scatter | solution.py:191
  89.2 41.4 %copy-start = (f32[512,1536]{1,0:T(8,128)}, f32[512,1536]{1,0:T(8,128)S(1)}, u32[]{:S(2)}) copy-start(f32[512,1536]{1,0:T(8,128)S(1)} %fusion.12) | copy-start | bytes 9437188
  132.0 1.7 copy-start.9
  133.5 1.2 copy-start.8
  135.1 1.7 copy-start.14
  136.8 1.7 copy-start.10
  139.1 13.3 %copy-start.5 = (bf16[4,128,12,64]{1,0,3,2:T(4,128)(2,1)}, bf16[4,128,12,64]{1,0,3,2:T(4,128)(2,1)S(1)}, u32[]{:S(2)}) copy-start(bf16[4,128,12,64]{1,0,3,2:T(4,128)(2,1)S(1)} %copy.70) | copy-start | bytes 2359300
  152.4 119.8 %copy-start.7 = (bf16[512,768]{1,0:T(8,128)(2,1)}, bf16[512,768]{1,0:T(8,128)(2,1)S(1)}, u32[]{:S(2)}) copy-start(bf16[512,768]{1,0:T(8,128)(2,1)S(1)} %get-tuple-element.50) | copy-start | bytes 2359300
  254.8 7.0 %copy-start.1 = (f32[512,1536]{1,0:T(8,128)S(1)}, f32[512,1536]{1,0:T(8,128)}, u32[]{:S(2)}) copy-start(f32[512,1536]{1,0:T(8,128)} %copy-done) | copy-start | bytes 9437188
  254.8 9.4 %copy-start.29 = (f32[512,3072]{1,0:T(8,128)S(1)}, f32[512,3072]{1,0:T(8,128)}, u32[]{:S(2)}) copy-start(f32[512,3072]{1,0:T(8,128)} %get-tuple-element.52) | copy-start | bytes 18874372
  261.8 2.4 copy-start.27
  262.7 6.3 slice-start
  264.2 4.8 copy-start.12
  264.2 4.8 slice-start.1
  268.9 3.3 copy-start.30
  272.3 1.8 copy-start.28
  272.9 1.1 copy-start.3
  275.3 3.4 copy-start.11
  275.4 3.4 copy-start.15
  284.3 2.7 copy-start.2
  284.7 1.4 copy-start.16
  291.2 98.7 %reduce-scatter.9.cloned.1.call-start = ((), (), s32[]{:S(2)}) async-start(), calls=%async_computation.13 | async-start | bytes 5308416 | tf_op jit(solution)/shard_map/reduce_scatter | solution.py:191
  298.4 1.4 copy-start.13
  298.4 147.2 %reduce-scatter.11.cloned.1.call-start = ((), (), s32[]{:S(2)}) async-start(), calls=%async_computation.14 | async-start | bytes 5308416 | tf_op jit(solution)/shard_map/reduce_scatter | solution.py:191
  306.5 1.4 copy-start.4
  306.5 1.6 copy-start.6
  306.5 186.6 %reduce-scatter.7.cloned.1.call-start = ((), (), s32[]{:S(2)}) async-start(), calls=%async_computation.12 | async-start | bytes 1327104 | tf_op jit(solution)/shard_map/reduce_scatter | solution.py:191
  309.9 216.6 %all-gather.30.cloned.1.call-start = ((), (), s32[]{:S(2)}) async-start(), calls=%async_computation.10 | async-start | bytes 3932160 | tf_op jit(solution)/shard_map/all_gather | solution.py:187
  315.7 257.4 %all-gather.28.cloned.1.call-start = ((), (), s32[]{:S(2)}) async-start(), calls=%async_computation.9 | async-start | bytes 3932160 | tf_op jit(solution)/shard_map/all_gather | solution.py:135
  316.4 291.1 %all-gather.32.cloned.1.call-start = ((), (), s32[]{:S(2)}) async-start(), calls=%async_computation.15 | async-start | bytes 2211840 | tf_op jit(solution)/shard_map/all_gather | solution.py:192
  334.0 313.1 %all-gather.34.cloned.1.call-start = ((), (), s32[]{:S(2)}) async-start(), calls=%async_computation.16 | async-start | bytes 2949120 | tf_op jit(solution)/shard_map/all_gather | solution.py:192
  389.9 296.5 %all-gather.36.cloned.1.call-start = ((), (), s32[]{:S(2)}) async-start(), calls=%async_computation.17 | async-start | bytes 2949120 | tf_op jit(solution)/shard_map/all_gather | solution.py:192
Sparse Core Ops, SparseCore 0:
  10.4 72.8 all-gather.17
  85.0 41.5 all-gather.19
  128.2 21.5 all-gather.21
  151.2 51.4 all-gather.23
  204.2 50.5 all-gather.25
  291.3 42.6 reduce-scatter.4
  336.4 53.4 reduce-scatter.8
  392.3 53.3 reduce-scatter.10
  448.6 31.4 reduce-scatter.6
  482.5 43.9 all-gather.29
  529.1 43.9 all-gather.27
  574.9 32.5 all-gather.31
  609.5 37.4 all-gather.33
  648.9 37.4 all-gather.35
